TPU v7x, 32 devices: a whole 2x2x4 slice. The times are simulated.
32 devices in a mesh: rows: 16 (over z, y, x), heads: 2 (over core).
Axes of the slice: x: 2, y: 2, z: 4, core: 2. Of those that a mesh axis runs over, the one named last changes fastest.
Arguments:
- tokens: bfloat16 [49152, 768], P('rows'), may hold values from -6 to 6
- cotangent: bfloat16 [49152, 768], P(('rows', 'heads')), may hold values from -6 to 6
- lengths: int32 [96], P('rows'), may hold values from 1 to 512, 29491 in all
- qkv_weight: float32 [3, 768, 768], P(None, 'rows', 'heads'), may hold values from -0.3125 to 0.3125
- qkv_first: float32 [3, 768, 768], P(None, 'rows', 'heads'), may hold values from -0.0625 to 0.0625
- qkv_second: float32 [3, 768, 768], P(None, 'rows', 'heads'), may hold values from 1.4e-06 to 5.7e-06
- out_weight: float32 [768, 768], P(('rows', 'heads')), may hold values from -0.625 to 0.625
- out_first: float32 [768, 768], P(('rows', 'heads')), may hold values from -0.0625 to 0.0625
- out_second: float32 [768, 768], P(('rows', 'heads')), may hold values from 1.4e-06 to 5.7e-06
- in_weight: float32 [768, 3072], P(('rows', 'heads')), may hold values from -0.21875 to 0.21875
- in_first: float32 [768, 3072], P(('rows', 'heads')), may hold values from -0.0625 to 0.0625
- in_second: float32 [768, 3072], P(('rows', 'heads')), may hold values from 1.4e-06 to 5.7e-06
- back_weight: float32 [3072, 768], P(('rows', 'heads')), may hold values from -0.109375 to 0.109375
- back_first: float32 [3072, 768], P(('rows', 'heads')), may hold values from -0.0625 to 0.0625
- back_second: float32 [3072, 768], P(('rows', 'heads')), may hold values from 1.4e-06 to 5.7e-06
- vectors: float32 [12, 768], replicated, may hold values from -0.8 to 1.8, as said below
- vector_first: float32 [12, 768], replicated, may hold values from -0.0625 to 0.0625
- vector_second: float32 [12, 768], replicated, may hold values from 1.4e-06 to 5.7e-06
Outputs:
- block_out: float32 [49152, 768], P(('rows', 'heads'))
- grad_in: float32 [49152, 768], P(('rows', 'heads'))
- grad_norm: float32 [1], replicated
- qkv_new: float32 [3, 768, 768], P(None, 'rows', 'heads')
- qkv_first_new: float32 [3, 768, 768], P(None, 'rows', 'heads')
- qkv_second_new: float32 [3, 768, 768], P(None, 'rows', 'heads')
- out_new: float32 [768, 768], P(('rows', 'heads'))
- out_first_new: float32 [768, 768], P(('rows', 'heads'))
- out_second_new: float32 [768, 768], P(('rows', 'heads'))
- in_new: float32 [768, 3072], P(('rows', 'heads'))
- in_first_new: float32 [768, 3072], P(('rows', 'heads'))
- in_second_new: float32 [768, 3072], P(('rows', 'heads'))
- back_new: float32 [3072, 768], P(('rows', 'heads'))
- back_first_new: float32 [3072, 768], P(('rows', 'heads'))
- back_second_new: float32 [3072, 768], P(('rows', 'heads'))
- vectors_new: float32 [12, 768], replicated
- vector_first_new: float32 [12, 768], replicated
- vector_second_new: float32 [12, 768], replicated
Inputs may be any that keep to these rules, and one draw needn't show every extreme that they name: Each sequence's keys at positions lengths[i] and beyond are masked; the longest sequence has exactly 512. `vectors`: rows 3 and 6 are the norms' gains, the other rows biases.
All inputs are finite; a program needn't handle non-finite values. No bound on the sum of `lengths` on one device may be relied on, other than what follows from the above.
Results may differ from a plain program's by a relative error of at most 0.015.
The roundings to bfloat16 on the way count: a program that leaves them out, or rounds other values in their place, can miss the bound.
Values may be sent and summed in bfloat16 or wider, within the bound.
No kernel may reach another device: no remote copies, remote signals or barrier semaphores. Data moves between devices by JAX's collectives and lax.ppermute only.
A program may use at most 192 MiB of HBM per device.

v0:
```python
import jax
import jax.numpy as jnp
from jax import lax
from jax.sharding import PartitionSpec as P

HEAD_DIM = 64
eps_norm = 1e-12
clip_limit = 100.0
learn_rate = 0.08
vector_rate = 0.3
beta_one = 0.9
beta_two = 0.999
adam_eps = 1e-06
decay_rate = 0.01
step_count = 10


def layer_norm(values, gain, shift):
    center = values - jnp.mean(values, axis=-1, keepdims=True)
    spread = jnp.mean(center * center, axis=-1, keepdims=True)
    return center * lax.rsqrt(spread + eps_norm) * gain + shift


def gelu_exact(values):
    return jax.nn.gelu(values, approximate=False)


def masked_scores(queries, key_rows, length):
    scores = jnp.einsum(
        "qhe,khe->hqk", queries, key_rows, preferred_element_type=jnp.float32
    ) * HEAD_DIM ** (-0.5)
    places = lax.broadcasted_iota(jnp.int32, (1, 1, scores.shape[2]), 2)
    return jnp.where(places < length, scores, -1000000000.0)


def attend_forward(item):
    queries, key_rows, value_rows, length = item
    scores = masked_scores(queries, key_rows, length)
    highest = jnp.max(scores, axis=2, keepdims=True)
    weights = jnp.exp(scores - highest)
    total = jnp.sum(weights, axis=2, keepdims=True)
    probs = (weights / total).astype(jnp.bfloat16)
    context = jnp.einsum("hqk,khe->qhe", probs, value_rows, preferred_element_type=jnp.float32)
    return (context.astype(jnp.bfloat16), highest + jnp.log(total))


def attend_backward(item):
    queries, key_rows, value_rows, length, log_total, grad_context = item
    scores = masked_scores(queries, key_rows, length)
    probs = jnp.exp(scores - log_total)
    grad_value = jnp.einsum(
        "hqk,qhe->khe", probs.astype(jnp.bfloat16), grad_context, preferred_element_type=jnp.float32
    )
    grad_probs = jnp.einsum(
        "qhe,khe->hqk", grad_context, value_rows, preferred_element_type=jnp.float32
    )
    grad_scores = probs * (grad_probs - jnp.sum(probs * grad_probs, axis=2, keepdims=True))
    grad_scores = grad_scores.astype(jnp.bfloat16)
    scaling = HEAD_DIM ** (-0.5)
    grad_query = (
        jnp.einsum("hqk,khe->qhe", grad_scores, key_rows, preferred_element_type=jnp.float32)
        * scaling
    )
    grad_key = (
        jnp.einsum("hqk,qhe->khe", grad_scores, queries, preferred_element_type=jnp.float32)
        * scaling
    )
    return (
        grad_query.astype(jnp.bfloat16),
        grad_key.astype(jnp.bfloat16),
        grad_value.astype(jnp.bfloat16),
    )


def adam_update(weight, first, second, grad, decay, rate):
    first_new = beta_one * first + (1.0 - beta_one) * grad
    second_new = beta_two * second + (1.0 - beta_two) * grad * grad
    fix_one = 1.0 - beta_one**step_count
    fix_two = 1.0 - beta_two**step_count
    move = first_new / fix_one / (jnp.sqrt(second_new / fix_two) + adam_eps)
    return (weight - rate * (move + decay * weight), first_new, second_new)


def body(
    tokens,
    cotangent,
    lengths,
    qkv_weight,
    qkv_first,
    qkv_second,
    out_weight,
    out_first,
    out_second,
    in_weight,
    in_first,
    in_second,
    back_weight,
    back_first,
    back_second,
    vectors,
    vector_first,
    vector_second,
):
    head_index = lax.axis_index("heads")
    local = qkv_weight.shape[2]
    model = tokens.shape[1]
    tok_all = tokens.shape[0]
    tok_half = cotangent.shape[0]
    seq_count = lengths.shape[0]
    seq_len = tok_all // seq_count
    loc_heads = local // HEAD_DIM
    qkv_full = lax.all_gather(qkv_weight.astype(jnp.bfloat16), "rows", axis=1, tiled=True)
    out_full, in_full, back_full = (
        lax.all_gather(out_weight.astype(jnp.bfloat16), ("rows", "heads"), axis=0, tiled=True),
        lax.all_gather(in_weight.astype(jnp.bfloat16), ("rows", "heads"), axis=0, tiled=True),
        lax.all_gather(back_weight.astype(jnp.bfloat16), ("rows", "heads"), axis=0, tiled=True),
    )
    bias_query = lax.dynamic_slice_in_dim(vectors[0], head_index * local, local)
    bias_value = lax.dynamic_slice_in_dim(vectors[1], head_index * local, local)
    bias_inner = vectors[8:].reshape(-1)
    projected = jnp.einsum("td,jdc->jtc", tokens, qkv_full, preferred_element_type=jnp.float32)
    queries = (projected[0] + bias_query).astype(jnp.bfloat16)
    key_rows = projected[1].astype(jnp.bfloat16)
    value_rows = (projected[2] + bias_value).astype(jnp.bfloat16)

    def per_seq(array):
        return array.reshape(seq_count, seq_len, loc_heads, HEAD_DIM)

    seq_query = per_seq(queries)
    seq_key = per_seq(key_rows)
    seq_value = per_seq(value_rows)
    context, log_totals = lax.map(attend_forward, (seq_query, seq_key, seq_value, lengths))
    context = context.reshape(tok_all, local)
    ctx_tokens = lax.all_to_all(context, "heads", split_axis=0, concat_axis=1, tiled=True)
    x_half = lax.dynamic_slice_in_dim(tokens, head_index * tok_half, tok_half, 0).astype(
        jnp.float32
    )
    attn_out = jnp.dot(ctx_tokens, out_full, preferred_element_type=jnp.float32) + vectors[2]
    hidden, norm_one_pull = jax.vjp(layer_norm, x_half + attn_out, vectors[3], vectors[4])
    hidden_low = hidden.astype(jnp.bfloat16)
    inner = jnp.dot(hidden_low, in_full, preferred_element_type=jnp.float32) + bias_inner
    activ, gelu_pull = jax.vjp(gelu_exact, inner)
    activ_low = activ.astype(jnp.bfloat16)
    ffn_out = jnp.dot(activ_low, back_full, preferred_element_type=jnp.float32) + vectors[5]
    block_out, norm_two_pull = jax.vjp(layer_norm, hidden + ffn_out, vectors[6], vectors[7])
    grad_second, grad_gain_two, grad_shift_two = norm_two_pull(cotangent.astype(jnp.float32))
    grad_ffn = grad_second.astype(jnp.bfloat16)
    grad_back = jnp.dot(activ_low.T, grad_ffn, preferred_element_type=jnp.float32)
    grad_activ = jnp.dot(grad_ffn, back_full.T, preferred_element_type=jnp.float32)
    grad_inner = gelu_pull(grad_activ)[0].astype(jnp.bfloat16)
    grad_in_w = jnp.dot(hidden_low.T, grad_inner, preferred_element_type=jnp.float32)
    grad_hidden = grad_second + jnp.dot(grad_inner, in_full.T, preferred_element_type=jnp.float32)
    grad_first, grad_gain_one, grad_shift_one = norm_one_pull(grad_hidden)
    grad_attn = grad_first.astype(jnp.bfloat16)
    grad_out_w = jnp.dot(ctx_tokens.T, grad_attn, preferred_element_type=jnp.float32)
    grad_ctx = jnp.dot(grad_attn, out_full.T, preferred_element_type=jnp.float32).astype(
        jnp.bfloat16
    )
    grad_context = lax.all_to_all(grad_ctx, "heads", split_axis=1, concat_axis=0, tiled=True)
    grad_query, grad_key, grad_value = lax.map(
        attend_backward, (seq_query, seq_key, seq_value, lengths, log_totals, per_seq(grad_context))
    )
    grad_stack = jnp.stack(
        [
            grad_query.reshape(tok_all, local),
            grad_key.reshape(tok_all, local),
            grad_value.reshape(tok_all, local),
        ]
    )
    grad_qkv = jnp.einsum("td,jtc->jdc", tokens, grad_stack, preferred_element_type=jnp.float32)
    grad_tokens = jnp.einsum(
        "jtc,jdc->td", grad_stack, qkv_full, preferred_element_type=jnp.float32
    )
    grad_in = grad_first + lax.psum_scatter(
        grad_tokens.astype(jnp.bfloat16), "heads", scatter_dimension=0, tiled=True
    ).astype(jnp.float32)
    qkv_grad = lax.psum_scatter(grad_qkv, "rows", scatter_dimension=1, tiled=True)
    out_grad, in_grad, back_grad = (
        lax.psum_scatter(grad_out_w, ("rows", "heads"), scatter_dimension=0, tiled=True),
        lax.psum_scatter(grad_in_w, ("rows", "heads"), scatter_dimension=0, tiled=True),
        lax.psum_scatter(grad_back, ("rows", "heads"), scatter_dimension=0, tiled=True),
    )
    zero_row = jnp.zeros((model,), jnp.float32)
    row_query = lax.dynamic_update_slice_in_dim(
        zero_row, jnp.sum(grad_stack[0].astype(jnp.float32), axis=0), head_index * local, 0
    )
    row_value = lax.dynamic_update_slice_in_dim(
        zero_row, jnp.sum(grad_stack[2].astype(jnp.float32), axis=0), head_index * local, 0
    )
    vector_part = jnp.concatenate(
        [
            row_query[None],
            row_value[None],
            jnp.sum(grad_attn.astype(jnp.float32), axis=0)[None],
            grad_gain_one[None],
            grad_shift_one[None],
            jnp.sum(grad_ffn.astype(jnp.float32), axis=0)[None],
            grad_gain_two[None],
            grad_shift_two[None],
            jnp.sum(grad_inner.astype(jnp.float32), axis=0).reshape(-1, model),
        ],
        axis=0,
    )
    square_part = (
        jnp.sum(qkv_grad * qkv_grad)
        + jnp.sum(out_grad * out_grad)
        + jnp.sum(in_grad * in_grad)
        + jnp.sum(back_grad * back_grad)
    )
    vector_grad, square_total = lax.psum((vector_part, square_part), ("rows", "heads"))
    grad_norm = jnp.sqrt(square_total + jnp.sum(vector_grad * vector_grad))
    factor = clip_limit / jnp.maximum(grad_norm, clip_limit)
    qkv_new = adam_update(
        qkv_weight, qkv_first, qkv_second, factor * qkv_grad, decay_rate, learn_rate
    )
    out_new = adam_update(
        out_weight, out_first, out_second, factor * out_grad, decay_rate, learn_rate
    )
    in_new = adam_update(in_weight, in_first, in_second, factor * in_grad, decay_rate, learn_rate)
    back_new = adam_update(
        back_weight, back_first, back_second, factor * back_grad, decay_rate, learn_rate
    )
    vec_new = adam_update(
        vectors, vector_first, vector_second, factor * vector_grad, 0.0, vector_rate
    )
    return (
        block_out,
        grad_in,
        grad_norm.reshape(1),
        qkv_new[0],
        qkv_new[1],
        qkv_new[2],
        out_new[0],
        out_new[1],
        out_new[2],
        in_new[0],
        in_new[1],
        in_new[2],
        back_new[0],
        back_new[1],
        back_new[2],
        vec_new[0],
        vec_new[1],
        vec_new[2],
    )


def solution(mesh):
    in_specs = (
        P("rows", None),
        P(("rows", "heads"), None),
        P("rows"),
        P(None, "rows", "heads"),
        P(None, "rows", "heads"),
        P(None, "rows", "heads"),
        P(("rows", "heads"), None),
        P(("rows", "heads"), None),
        P(("rows", "heads"), None),
        P(("rows", "heads"), None),
        P(("rows", "heads"), None),
        P(("rows", "heads"), None),
        P(("rows", "heads"), None),
        P(("rows", "heads"), None),
        P(("rows", "heads"), None),
        P(),
        P(),
        P(),
    )
    out_specs = (
        P(("rows", "heads"), None),
        P(("rows", "heads"), None),
        P(),
        P(None, "rows", "heads"),
        P(None, "rows", "heads"),
        P(None, "rows", "heads"),
        P(("rows", "heads"), None),
        P(("rows", "heads"), None),
        P(("rows", "heads"), None),
        P(("rows", "heads"), None),
        P(("rows", "heads"), None),
        P(("rows", "heads"), None),
        P(("rows", "heads"), None),
        P(("rows", "heads"), None),
        P(("rows", "heads"), None),
        P(),
        P(),
        P(),
    )
    return jax.shard_map(body, mesh=mesh, in_specs=in_specs, out_specs=out_specs, check_vma=False)
```

profile of v0, /device:TPU:0, one launch (start us, length us, event | category | flops | bytes accessed | tf_op | source)
XLA Modules:
  0.0 1076.9 jit_solution(10501911551029216793)
XLA Ops:
  20.1 4.3 copy.140
  24.4 48.6 %all-gather.5.cloned.1.call-done = bf16[3,768,384]{2,1,0:T(8,128)(2,1)} async-done(((bf16[3,48,384]{2,1,0:T(8,128)(2,1)}), bf16[3,768,384]{2,1,0:T(8,128)(2,1)}) %all-gather.5.cloned.1.call-update) | async-done | bytes 1769488 | tf_op jit(solution)/shard_map/all_gather | solution.py:112
  73.0 8.2 convolution_bitcast_fusion
  81.2 4.4 fusion.95
  87.3 7.4 squeeze.40
  94.7 3.1 add_convert_fusion.2
  100.0 7.4 squeeze.41
  107.4 3.1 add_convert_fusion.1
  111.3 6.0 convert_element_type.109
  117.4 4.1 copy.137
  123.2 55.7 %while.26 = (s32[]{:T(128)}, bf16[6,512,6,64]{1,3,2,0:T(8,128)(2,1)}, f32[6,6,512,1]{2,1,3,0:T(8,128)}, bf16[6,512,6,64]{1,3,2,0:T(8,128)(2,1)}, s32[6]{0:T(128)...) while((s32[]{:T(128)}, bf16[6,512,6,64]{1,3,2,0:T(8,128)(2,1)}, ...), condition=%wide.region_3.4_spmd, body=%wide.region_0.3_spmd.sunk | while | flops 421721600 | bytes 20554340 | solution.py:132
  129.1 3.5 fusion.143
  138.3 3.5 fusion.143
  147.5 3.5 fusion.143
  156.8 3.5 fusion.143
  166.0 3.5 fusion.143
  175.2 3.6 fusion.143
  178.8 5.7 copy.138
  184.5 6.8 all_to_all.26
  191.3 3.3 copy.139
  194.7 5.0 all-to-all-start
  202.9 4.4 fusion.96
  210.3 49.8 %multiply_convert_fusion.1 = (bf16[1536,3072]{1,0:T(8,128)(2,1)}, f32[1536,3072]{1,0:T(8,128)}, f32[1536,3072]{1,0:T(8,128)}) fusion(f32[3072]{0:T(1024)S(1)} %add.251, bf16[768,3072]{1,0:T(8,128)(2,1)} %all-gather.9.cloned.1.call-done, bf16[1536,768]{0,1:T(8,128)(2,1)S(1)} %fusion.86.clone.4), kind=kOutput, calls=%fused_computation.68 | convolution fusion | flops 7559184384 | bytes 54276096 | tf_op jit(solution)/shard_map/dot_general | solution.py:141
  261.3 13.6 %fusion.97 = (f32[1536]{0:T(1024)S(1)}, f32[1536,768]{0,1:T(8,128)S(1)}) fusion(f32[768]{0:T(1024)S(1)} %copy-done.36, bf16[1536,3072]{1,0:T(8,128)(2,1)} %get-tuple-element.328, bf16[3072,768]{1,0:T(8,128)(2,1)} %all-gather.11.cloned.1.call-done, f32[768]{0:T(1024)S(1)} %get-tuple-element.265, f32[768]{0:T(1024)S(1)} %get-tuple-element.266, ...), kind=kOutput, calls=%fused_computation.175 | convolution fusion | flops 7256013312 | bytes 23620608 | tf_op jit(solution)/shard_map/dot_general | solution.py:144
  280.2 5.4 convert_reduce_fusion.2
  285.6 26.8 %convert_reduce_fusion = (f32[3072]{0:T(1024)}, bf16[1536,3072]{1,0:T(8,128)(2,1)}) fusion(f32[1536,3072]{1,0:T(8,128)} %get-tuple-element.329, bf16[1536,768]{0,1:T(8,128)(2,1)} %get-tuple-element.321, bf16[3072,768]{1,0:T(8,128)(2,1)} %all-gather.11.cloned.1.call-done, f32[1536,3072]{1,0:T(8,128)} %get-tuple-element.343, f32[3072]{0:T(1024)S(1)} %add.251), kind=kOutput, calls=%fused_computation.66 | convolution fusion | flops 7327970304 | bytes 54288384 | tf_op jit(solution)/shard_map/dot_general | solution.py:149
  312.4 14.9 %multiply_reduce_fusion.1 = (f32[768]{0:T(1024)}, f32[1536]{0:T(1024)S(1)}, f32[768]{0:T(1024)}, f32[1536,768]{0,1:T(8,128)S(1)}) fusion(f32[1536,768]{0,1:T(8,128)S(1)} %bitcast.160, f32[1536]{0:T(1024)S(1)} %fusion.81, f32[1536]{0:T(1024)S(1)} %broadcast_multiply_fusion.1, f32[768]{0:T(1024)S(1)} %get-tuple-element.266, ...), kind=kOutput, calls=%fused_computation.100 | convolution fusion | flops 7267808256 | bytes 30726144 | tf_op jit(solution)/shard_map/dot_general | solution.py:152
  331.9 5.1 fusion.98
  337.0 3.3 convolution_convert_fusion
  340.3 5.6 all_to_all.35
  345.9 3.8 copy.142
  349.7 5.7 reshape.186
  361.3 104.7 %while.27 = (s32[]{:T(128)}, bf16[6,512,6,64]{1,3,2,0:T(8,128)(2,1)S(1)}, bf16[6,512,6,64]{1,3,2,0:T(8,128)(2,1)}, bf16[6,512,6,64]{1,3,2,0:T(8,128)(2,1)}, bf16...) while((s32[]{:T(128)}, ...), condition=%wide.region_14.15_spmd, body=%wide.region_12.14_spmd.sunk | while | flops 1031206400 | bytes 51211392 | solution.py:160
  365.7 3.3 multiply_reduce_fusion.11
  375.6 3.4 fusion.155
  383.1 3.3 multiply_reduce_fusion.11
  393.0 3.4 fusion.155
  400.5 3.3 multiply_reduce_fusion.11
  410.4 3.4 fusion.155
  417.9 3.3 multiply_reduce_fusion.11
  427.8 3.4 fusion.155
  435.3 3.3 multiply_reduce_fusion.11
  445.2 3.4 fusion.155
  452.7 3.3 multiply_reduce_fusion.11
  462.6 3.4 fusion.155
  466.0 6.0 copy.166
  472.0 8.7 reshape.195
  480.7 7.7 copy.167
  488.4 8.7 reshape.196
  497.2 7.7 copy.168
  504.8 9.1 reshape.197
  520.5 7.7 fusion.73
  528.1 6.3 copy.155
  534.5 10.5 bitcast_convert_fusion
  545.7 13.8 %fusion.83 = f32[768,3072]{1,0:T(8,128)} fusion(bf16[1536,3072]{1,0:T(8,128)(2,1)} %get-tuple-element.348, f32[1536,768]{0,1:T(8,128)} %copy-done.1, f32[768]{0:T(1024)S(1)} %copy-done.30, f32[768]{0:T(1024)S(1)} %get-tuple-element.266, f32[1536]{0:T(1024)S(1)} %fusion.81, f32[1536]{0:T(1024)S(1)} %broadcast_multiply_fusion.1), kind=kOutput, calls=%fused_computation.169 | convolution fusion | flops 7253655552 | bytes 23611392 | tf_op jit(solution)/shard_map/dot_general | solution.py:151
  559.6 13.3 %fusion.99 = f32[3072,768]{1,0:T(8,128)} fusion(bf16[1536,3072]{1,0:T(8,128)(2,1)} %get-tuple-element.328, bf16[1536,768]{0,1:T(8,128)(2,1)} %get-tuple-element.321), kind=kOutput, calls=%fused_computation.177 | convolution fusion | flops 7247757312 | bytes 21233664 | tf_op jit(solution)/shard_map/dot_general | solution.py:148
  577.6 6.1 copy.157
  585.3 127.9 %all-reduce.4.cloned.1.call-done = f32[3,768,384]{2,0,1:T(4,128)} async-done(((f32[3,768,384]{2,0,1:T(4,128)}), f32[3,768,384]{2,0,1:T(4,128)}) %all-reduce.4.cloned.1.call-update) | async-done | bytes 3538960
  716.2 11.0 %reduce-scatter.5.cloned.1.call-done = bf16[1536,768]{0,1:T(8,128)(2,1)} async-done(((bf16[3072,768]{0,1:T(8,128)(2,1)}), bf16[1536,768]{0,1:T(8,128)(2,1)}) %reduce-scatter.5.cloned.1.call-update) | async-done | bytes 2359312 | tf_op jit(solution)/shard_map/reduce_scatter | solution.py:174
  727.2 6.0 convert_add_fusion
  733.2 137.7 %reduce-scatter.9.cloned.1.call-done = f32[24,3072]{1,0:T(8,128)} async-done(((f32[768,3072]{1,0:T(8,128)}), f32[24,3072]{1,0:T(8,128)}) %reduce-scatter.9.cloned.1.call-update) | async-done | bytes 294928 | tf_op jit(solution)/shard_map/reduce_scatter | solution.py:180
  873.2 138.3 %reduce-scatter.11.cloned.1.call-done = f32[96,768]{1,0:T(8,128)} async-done(((f32[3072,768]{1,0:T(8,128)}), f32[96,768]{1,0:T(8,128)}) %reduce-scatter.11.cloned.1.call-update) | async-done | bytes 294928 | tf_op jit(solution)/shard_map/reduce_scatter | solution.py:181
  1013.9 6.2 copy.158
  1020.1 40.7 %all-reduce.1 = (f32[]{:T(128)}, f32[12,768]{1,0:T(8,128)}) all-reduce(f32[]{:T(128)S(6)} %add.266, f32[12,768]{1,0:T(8,128)S(1)} %concatenate.3), channel_id=1, replica_groups=mesh['rows'=16,'heads'=2] {'rows','heads'}, use_global_device_ids=true, to_apply=%region_24.25 | all-reduce | flops 9217 | bytes 73736 | tf_op jit(solution)/shard_map/psum | solution.py:210
  (254 shorter events, 165.7 us)
Async XLA Ops:
  7.2 65.8 %all-gather.5.cloned.1.call-start = ((), (), s32[]{:S(2)}) async-start(), calls=%async_computation.6 | async-start | bytes 1880064 | tf_op jit(solution)/shard_map/all_gather | solution.py:112
  8.9 190.9 %all-gather.7.cloned.1.call-start = ((), (), s32[]{:S(2)}) async-start(), calls=%async_computation.7 | async-start | bytes 1216512 | tf_op jit(solution)/shard_map/all_gather | solution.py:114
  10.4 199.9 %all-gather.9.cloned.1.call-start = ((), (), s32[]{:S(2)}) async-start(), calls=%async_computation.8 | async-start | bytes 4866048 | tf_op jit(solution)/shard_map/all_gather | solution.py:115
  12.2 249.2 %all-gather.11.cloned.1.call-start = ((), (), s32[]{:S(2)}) async-start(), calls=%async_computation.9 | async-start | bytes 4866048 | tf_op jit(solution)/shard_map/all_gather | solution.py:116
  15.6 245.8 %copy-start.29 = (f32[768]{0:T(1024)}, f32[768]{0:T(1024)S(1)}, u32[]{:S(2)}) copy-start(f32[768]{0:T(1024)S(1)} %get-tuple-element.265) | copy-start | bytes 9220
  15.8 4.3 slice-start.4
  117.3 5.8 copy-start.39
  178.8 12.5 %copy-start.3 = (bf16[6,512,6,64]{1,3,2,0:T(8,128)(2,1)}, bf16[6,512,6,64]{1,3,2,0:T(8,128)(2,1)S(1)}, u32[]{:S(2)}) copy-start(bf16[6,512,6,64]{1,3,2,0:T(8,128)(2,1)S(1)} %get-tuple-element.529) | copy-start | bytes 7077892
  194.7 8.2 copy-start.6
  194.7 8.2 all-to-all-start
  199.7 384.1 %reduce-scatter.7.cloned.1.call-start = ((), (), s32[]{:S(2)}) async-start(), calls=%async_computation.11 | async-start | bytes 2433024 | tf_op jit(solution)/shard_map/reduce_scatter | solution.py:179
  207.3 2.2 copy-start.1
  207.9 1.0 copy-start.21
  210.3 51.1 %copy-start.36 = (f32[768]{0:T(1024)S(1)}, f32[768]{0:T(1024)}, u32[]{:S(2)}) copy-start(f32[768]{0:T(1024)} %get-tuple-element.264) | copy-start | bytes 9220
  261.3 13.7 %copy-start.2 = (bf16[1536,768]{0,1:T(8,128)(2,1)S(1)}, bf16[1536,768]{0,1:T(8,128)(2,1)}, u32[]{:S(2)}) copy-start(bf16[1536,768]{0,1:T(8,128)(2,1)} %copy.140) | copy-start | bytes 7077892
  261.3 13.7 %copy-start.27 = (f32[768]{0:T(1024)S(1)}, f32[768]{0:T(1024)}, u32[]{:S(2)}) copy-start(f32[768]{0:T(1024)} %get-tuple-element.263) | copy-start | bytes 9220
  277.1 3.1 copy-start.31
  280.2 32.2 %slice-start = ((s8[4718592]{0:T(1024)(128)(4,1)}), s8[4194304]{0:T(1024)(128)(4,1)S(1)}, s32[]{:S(2)}) async-start(s8[4718592]{0:T(1024)(128)(4,1)} %bitcast.159), calls=%async_computation.15 | async-start | bytes 8388608
  285.6 26.8 %slice-start.1 = ((s8[4718592]{0:T(1024)(128)(4,1)}), s8[524288]{0:T(1024)(128)(4,1)S(1)}, s32[]{:S(2)}) async-start(s8[4718592]{0:T(1024)(128)(4,1)} %bitcast.159), calls=%async_computation.16 | async-start | bytes 1048576
  312.4 14.9 %copy-start.22 = (f32[1536]{0:T(1024)S(1)}, f32[1536]{0:T(1024)}, u32[]{:S(2)}) copy-start(f32[1536]{0:T(1024)} %copy-done.21) | copy-start | bytes 18436
  328.7 2.2 copy-start
  328.7 8.3 copy-start.25
  357.6 3.7 copy-start.40
  357.6 355.5 %all-reduce.4.cloned.1.call-start = ((), (), s32[]{:S(2)}) async-start(), calls=%async_computation.14 | async-start | bytes 9437184
  514.0 2.4 copy-start.4
  514.0 3.1 copy-start.5
  514.0 6.5 slice-start.2
  516.4 4.1 slice-start.3
  517.5 2.9 copy-start.12
  534.5 192.7 %reduce-scatter.5.cloned.1.call-start = ((), (), s32[]{:S(2)}) async-start(), calls=%async_computation.10 | async-start | bytes 7077888 | tf_op jit(solution)/shard_map/reduce_scatter | solution.py:174
  545.0 0.7 copy-start.30
  545.1 325.8 %reduce-scatter.9.cloned.1.call-start = ((), (), s32[]{:S(2)}) async-start(), calls=%async_computation.12 | async-start | bytes 9732096 | tf_op jit(solution)/shard_map/reduce_scatter | solution.py:180
  559.6 451.9 %reduce-scatter.11.cloned.1.call-start = ((), (), s32[]{:S(2)}) async-start(), calls=%async_computation.13 | async-start | bytes 9732096 | tf_op jit(solution)/shard_map/reduce_scatter | solution.py:181
  572.9 0.7 copy-start.41
  572.9 4.5 copy-start.34
  573.0 4.5 copy-start.38
  573.0 4.5 copy-start.37
  573.0 4.5 copy-start.35
  573.0 4.6 copy-start.33
  573.0 4.6 copy-start.32
  573.0 4.6 copy-start.28
  577.6 149.6 %copy-start.26 = (f32[1536]{0:T(1024)S(1)}, f32[1536]{0:T(1024)}, u32[]{:S(2)}) copy-start(f32[1536]{0:T(1024)} %copy-done.25) | copy-start | bytes 18436
  1013.8 51.5 %copy-start.11 = (f32[3,48,384]{2,1,0:T(8,128)S(1)}, f32[3,48,384]{2,1,0:T(8,128)}, u32[]{:S(2)}) copy-start(f32[3,48,384]{2,1,0:T(8,128)} %param.25) | copy-start | bytes 663556
  1013.8 51.5 %copy-start.19 = (f32[3,48,384]{2,1,0:T(8,128)S(1)}, f32[3,48,384]{2,1,0:T(8,128)}, u32[]{:S(2)}) copy-start(f32[3,48,384]{2,1,0:T(8,128)} %param.26) | copy-start | bytes 663556
  1013.8 51.5 %copy-start.20 = (f32[3,48,384]{2,1,0:T(8,128)S(1)}, f32[3,48,384]{2,1,0:T(8,128)}, u32[]{:S(2)}) copy-start(f32[3,48,384]{2,1,0:T(8,128)} %param.27) | copy-start | bytes 663556
  1013.8 52.4 %copy-start.7 = (f32[96,768]{1,0:T(8,128)S(1)}, f32[96,768]{1,0:T(8,128)}, u32[]{:S(2)}) copy-start(f32[96,768]{1,0:T(8,128)} %param.34) | copy-start | bytes 884740
  1013.8 52.4 %copy-start.10 = (f32[96,768]{1,0:T(8,128)S(1)}, f32[96,768]{1,0:T(8,128)}, u32[]{:S(2)}) copy-start(f32[96,768]{1,0:T(8,128)} %reduce-scatter.11.cloned.1.call-done) | copy-start | bytes 884740
  1013.8 52.4 %copy-start.13 = (f32[96,768]{1,0:T(8,128)S(1)}, f32[96,768]{1,0:T(8,128)}, u32[]{:S(2)}) copy-start(f32[96,768]{1,0:T(8,128)} %param.35) | copy-start | bytes 884740
  1013.8 52.4 %copy-start.14 = (f32[96,768]{1,0:T(8,128)S(1)}, f32[96,768]{1,0:T(8,128)}, u32[]{:S(2)}) copy-start(f32[96,768]{1,0:T(8,128)} %param.36) | copy-start | bytes 884740
  1013.8 53.5 %copy-start.8 = (f32[24,3072]{1,0:T(8,128)S(1)}, f32[24,3072]{1,0:T(8,128)}, u32[]{:S(2)}) copy-start(f32[24,3072]{1,0:T(8,128)} %param.31) | copy-start | bytes 884740
  1013.8 53.4 %copy-start.9 = (f32[24,3072]{1,0:T(8,128)S(1)}, f32[24,3072]{1,0:T(8,128)}, u32[]{:S(2)}) copy-start(f32[24,3072]{1,0:T(8,128)} %reduce-scatter.9.cloned.1.call-done) | copy-start | bytes 884740
  1013.9 53.4 %copy-start.15 = (f32[24,3072]{1,0:T(8,128)S(1)}, f32[24,3072]{1,0:T(8,128)}, u32[]{:S(2)}) copy-start(f32[24,3072]{1,0:T(8,128)} %param.32) | copy-start | bytes 884740
  1013.9 53.4 %copy-start.16 = (f32[24,3072]{1,0:T(8,128)S(1)}, f32[24,3072]{1,0:T(8,128)}, u32[]{:S(2)}) copy-start(f32[24,3072]{1,0:T(8,128)} %param.33) | copy-start | bytes 884740
  1020.1 48.3 %copy-start.17 = (f32[24,768]{1,0:T(8,128)S(1)}, f32[24,768]{1,0:T(8,128)}, u32[]{:S(2)}) copy-start(f32[24,768]{1,0:T(8,128)} %param.28) | copy-start | bytes 221188
  1020.1 48.3 %copy-start.18 = (f32[24,768]{1,0:T(8,128)S(1)}, f32[24,768]{1,0:T(8,128)}, u32[]{:S(2)}) copy-start(f32[24,768]{1,0:T(8,128)} %reduce-scatter.7.cloned.1.call-done) | copy-start | bytes 221188
  1060.8 7.6 copy-start.23
  1063.6 4.7 copy-start.24
Sparse Core Ops, SparseCore 0:
  11.3 61.6 all-gather.4
  76.4 52.7 all-gather.6
  132.8 62.5 all-gather.8
  198.7 62.6 all-gather.10
  357.8 97.8 reduce-scatter.6
  534.6 178.5 all-reduce.3
  715.5 11.6 reduce-scatter.4
  734.1 136.7 reduce-scatter.8
  876.8 134.5 reduce-scatter.10
where the time goes:
time: 1090 us; the launch traced here: 1080 us
  waiting for transfers between devices  468 us (43%)
  matrix products  287 us (26%)
  local copies, waits for them, and re-layouts  168 us (15%)
  other arithmetic  81.8 us (8%)
  blocking collectives  46.3 us (4%)
  between operations  20.4 us (2%)
    reduce_scatter x1, waiting for transfers between devices, body(): lax.psum_scatter(grad_back, ('rows', 'heads'), scatter_dimension=0, tiled...  138 us
    reduce_scatter x1, waiting for transfers between devices, body(): lax.psum_scatter(grad_in_w, ('rows', 'heads'), scatter_dimension=0, tiled...  138 us
    unnamed x10, waiting for transfers between devices  128 us
    dot_general x1, matrix products, body(): jnp.dot(hidden_low, in_full, preferred_element_type=jnp.float32)  49.8 us
    all_gather x1, waiting for transfers between devices, body(): lax.all_gather(qkv_weight.astype(jnp.bfloat16), 'rows', axis=1, tiled=True)  48.6 us
    another operation x7, local copies, waits for them, and re-layouts, body(): jnp.stack([grad_query.reshape(tok_all, local), grad_key.reshape(tok_all,...  48.4 us
    psum x1, blocking collectives, body(): lax.psum((vector_part, square_part), ('rows', 'heads'))  40.7 us
    unnamed x99, local copies, waits for them, and re-layouts  30.7 us
  transfers between devices with their start and end apart: 10, of which 7 were waited for; matrix products, arithmetic and copies ran while one was open for 39% of the time, Pallas kernels for 0%

commit v1 on v0

--- a/solution.py
+++ b/solution.py
@@ -1,3 +1,4 @@
+import functools
 import jax
 import jax.numpy as jnp
 from jax import lax
@@ -13,6 +14,13 @@
 adam_eps = 1e-06
 decay_rate = 0.01
 step_count = 10
+
+
+def finish_classes_up(u_in, ax_name, comm_axis):
+    return jax.lax.psum(jax.lax.psum(u_in, axis_name=ax_name), axis_name=comm_axis)
+
+
+words_state = functools.partial(finish_classes_up, ax_name="heads", comm_axis="rows")
 
 
 def layer_norm(values, gain, shift):
@@ -207,7 +215,7 @@
         + jnp.sum(in_grad * in_grad)
         + jnp.sum(back_grad * back_grad)
     )
-    vector_grad, square_total = lax.psum((vector_part, square_part), ("rows", "heads"))
+    vector_grad, square_total = words_state((vector_part, square_part))
     grad_norm = jnp.sqrt(square_total + jnp.sum(vector_grad * vector_grad))
     factor = clip_limit / jnp.maximum(grad_norm, clip_limit)
     qkv_new = adam_update(

time: 1090 us -> 1130 us (1.037)
  blocking collectives: 46.3 us -> 85.3 us
    psum x1 -> x2, blocking collectives: 40.7 us -> 79.7 us  [the longest x1 75.5 us: finish_classes_up(): jax.lax.psum(jax.lax.psum(u_in, axis_name=ax_name), axis_name=comm_axis)]
  transfers between devices with their start and end apart: 10 -> 10, of which waited for: 7 -> 7; matrix products, arithmetic and copies ran while one was open for 39% -> 37% of each run, Pallas kernels for 0% -> 0%
where the time goes in v1:
time: 1130 us; the launch traced here: 1120 us
  waiting for transfers between devices  468 us (41%)
  matrix products  287 us (25%)
  local copies, waits for them, and re-layouts  168 us (15%)
  blocking collectives  85.3 us (8%)
  other arithmetic  80.9 us (7%)
  between operations  20.4 us (2%)
    reduce_scatter x1, waiting for transfers between devices, body(): lax.psum_scatter(grad_back, ('rows', 'heads'), scatter_dimension=0, tiled...  138 us
    reduce_scatter x1, waiting for transfers between devices, body(): lax.psum_scatter(grad_in_w, ('rows', 'heads'), scatter_dimension=0, tiled...  138 us
    unnamed x10, waiting for transfers between devices  128 us
    psum x1, blocking collectives, finish_classes_up(): jax.lax.psum(jax.lax.psum(u_in, axis_name=ax_name), axis_name=comm_axis)  75.5 us
    dot_general x1, matrix products, body(): jnp.dot(hidden_low, in_full, preferred_element_type=jnp.float32)  49.8 us
    all_gather x1, waiting for transfers between devices, body(): lax.all_gather(qkv_weight.astype(jnp.bfloat16), 'rows', axis=1, tiled=True)  48.6 us
    another operation x7, local copies, waits for them, and re-layouts, body(): jnp.stack([grad_query.reshape(tok_all, local), grad_key.reshape(tok_all,...  48.4 us
    unnamed x99, local copies, waits for them, and re-layouts  30.7 us
  transfers between devices with their start and end apart: 10, of which 7 were waited for; matrix products, arithmetic and copies ran while one was open for 37% of the time, Pallas kernels for 0%

profile of v1, /device:TPU:0, one launch (start us, length us, event | category | flops | bytes accessed | tf_op | source)
XLA Modules:
  0.0 1115.1 jit_solution(9641128455446315014)
XLA Ops:
  20.1 4.3 copy.140
  24.4 48.6 %all-gather.5.cloned.1.call-done = bf16[3,768,384]{2,1,0:T(8,128)(2,1)} async-done(((bf16[3,48,384]{2,1,0:T(8,128)(2,1)}), bf16[3,768,384]{2,1,0:T(8,128)(2,1)}) %all-gather.5.cloned.1.call-update) | async-done | bytes 1769488 | tf_op jit(solution)/shard_map/all_gather | solution.py:120
  73.0 8.2 convolution_bitcast_fusion
  81.2 4.4 fusion.95
  87.3 7.4 squeeze.40
  100.0 7.4 squeeze.41
  107.4 3.1 add_convert_fusion.1
  111.3 6.0 convert_element_type.109
  117.4 4.1 copy.137
  123.2 55.7 %while.26 = (s32[]{:T(128)}, bf16[6,512,6,64]{1,3,2,0:T(8,128)(2,1)}, f32[6,6,512,1]{2,1,3,0:T(8,128)}, bf16[6,512,6,64]{1,3,2,0:T(8,128)(2,1)}, s32[6]{0:T(128)...) while((s32[]{:T(128)}, bf16[6,512,6,64]{1,3,2,0:T(8,128)(2,1)}, ...), condition=%wide.region_3.4_spmd, body=%wide.region_0.3_spmd.sunk | while | flops 421721600 | bytes 20554340 | solution.py:140
  129.1 3.5 fusion.143
  138.3 3.5 fusion.143
  147.5 3.5 fusion.143
  156.8 3.5 fusion.143
  166.0 3.5 fusion.143
  175.2 3.6 fusion.143
  178.8 5.7 copy.138
  184.5 6.8 all_to_all.26
  191.3 3.3 copy.139
  194.7 5.0 all-to-all-start
  202.9 4.4 fusion.96
  210.3 49.8 %multiply_convert_fusion.1 = (bf16[1536,3072]{1,0:T(8,128)(2,1)}, f32[1536,3072]{1,0:T(8,128)}, f32[1536,3072]{1,0:T(8,128)}) fusion(f32[3072]{0:T(1024)S(1)} %add.255, bf16[768,3072]{1,0:T(8,128)(2,1)} %all-gather.9.cloned.1.call-done, bf16[1536,768]{0,1:T(8,128)(2,1)S(1)} %fusion.86.clone.4), kind=kOutput, calls=%fused_computation.68 | convolution fusion | flops 7559184384 | bytes 54276096 | tf_op jit(solution)/shard_map/dot_general | solution.py:149
  261.3 13.6 %fusion.97 = (f32[1536]{0:T(1024)S(1)}, f32[1536,768]{0,1:T(8,128)S(1)}) fusion(f32[768]{0:T(1024)S(1)} %copy-done.36, bf16[1536,3072]{1,0:T(8,128)(2,1)} %get-tuple-element.330, bf16[3072,768]{1,0:T(8,128)(2,1)} %all-gather.11.cloned.1.call-done, f32[768]{0:T(1024)S(1)} %get-tuple-element.265, f32[768]{0:T(1024)S(1)} %get-tuple-element.266, ...), kind=kOutput, calls=%fused_computation.175 | convolution fusion | flops 7256013312 | bytes 23620608 | tf_op jit(solution)/shard_map/dot_general | solution.py:152
  280.2 5.4 convert_reduce_fusion.2
  285.6 26.8 %convert_reduce_fusion = (f32[3072]{0:T(1024)}, bf16[1536,3072]{1,0:T(8,128)(2,1)}) fusion(f32[1536,3072]{1,0:T(8,128)} %get-tuple-element.331, bf16[1536,768]{0,1:T(8,128)(2,1)} %get-tuple-element.323, bf16[3072,768]{1,0:T(8,128)(2,1)} %all-gather.11.cloned.1.call-done, f32[1536,3072]{1,0:T(8,128)} %get-tuple-element.345, f32[3072]{0:T(1024)S(1)} %add.255), kind=kOutput, calls=%fused_computation.66 | convolution fusion | flops 7327970304 | bytes 54288384 | tf_op jit(solution)/shard_map/dot_general | solution.py:157
  312.4 14.9 %multiply_reduce_fusion.1 = (f32[768]{0:T(1024)}, f32[1536]{0:T(1024)S(1)}, f32[768]{0:T(1024)}, f32[1536,768]{0,1:T(8,128)S(1)}) fusion(f32[1536,768]{0,1:T(8,128)S(1)} %bitcast.160, f32[1536]{0:T(1024)S(1)} %fusion.81, f32[1536]{0:T(1024)S(1)} %broadcast_multiply_fusion.1, f32[768]{0:T(1024)S(1)} %get-tuple-element.266, ...), kind=kOutput, calls=%fused_computation.100 | convolution fusion | flops 7267808256 | bytes 30726144 | tf_op jit(solution)/shard_map/dot_general | solution.py:160
  331.9 5.1 fusion.98
  337.0 3.3 convolution_convert_fusion
  340.3 5.6 all_to_all.35
  345.9 3.8 copy.142
  349.7 5.7 reshape.186
  361.3 104.7 %while.27 = (s32[]{:T(128)}, bf16[6,512,6,64]{1,3,2,0:T(8,128)(2,1)S(1)}, bf16[6,512,6,64]{1,3,2,0:T(8,128)(2,1)}, bf16[6,512,6,64]{1,3,2,0:T(8,128)(2,1)}, bf16...) while((s32[]{:T(128)}, ...), condition=%wide.region_14.15_spmd, body=%wide.region_12.14_spmd.sunk | while | flops 1031206400 | bytes 51211392 | solution.py:168
  365.7 3.3 multiply_reduce_fusion.11
  375.6 3.4 fusion.155
  383.1 3.3 multiply_reduce_fusion.11
  393.0 3.4 fusion.155
  400.5 3.3 multiply_reduce_fusion.11
  410.4 3.4 fusion.155
  417.9 3.3 multiply_reduce_fusion.11
  427.8 3.4 fusion.155
  435.3 3.3 multiply_reduce_fusion.11
  445.2 3.4 fusion.155
  452.7 3.3 multiply_reduce_fusion.11
  462.6 3.4 fusion.155
  466.0 6.0 copy.166
  472.0 8.7 reshape.195
  480.7 7.7 copy.167
  488.4 8.7 reshape.196
  497.2 7.7 copy.168
  504.8 9.1 reshape.197
  520.5 7.7 fusion.73
  528.1 6.3 copy.155
  534.5 10.5 bitcast_convert_fusion
  545.7 13.8 %fusion.83 = f32[768,3072]{1,0:T(8,128)} fusion(bf16[1536,3072]{1,0:T(8,128)(2,1)} %get-tuple-element.350, f32[1536,768]{0,1:T(8,128)} %copy-done.1, f32[768]{0:T(1024)S(1)} %copy-done.30, f32[768]{0:T(1024)S(1)} %get-tuple-element.266, f32[1536]{0:T(1024)S(1)} %fusion.81, f32[1536]{0:T(1024)S(1)} %broadcast_multiply_fusion.1), kind=kOutput, calls=%fused_computation.169 | convolution fusion | flops 7253655552 | bytes 23611392 | tf_op jit(solution)/shard_map/dot_general | solution.py:159
  559.6 13.3 %fusion.99 = f32[3072,768]{1,0:T(8,128)} fusion(bf16[1536,3072]{1,0:T(8,128)(2,1)} %get-tuple-element.330, bf16[1536,768]{0,1:T(8,128)(2,1)} %get-tuple-element.323), kind=kOutput, calls=%fused_computation.177 | convolution fusion | flops 7247757312 | bytes 21233664 | tf_op jit(solution)/shard_map/dot_general | solution.py:156
  577.6 6.1 copy.157
  585.3 127.9 %all-reduce.5.cloned.1.call-done = f32[3,768,384]{2,0,1:T(4,128)} async-done(((f32[3,768,384]{2,0,1:T(4,128)}), f32[3,768,384]{2,0,1:T(4,128)}) %all-reduce.5.cloned.1.call-update) | async-done | bytes 3538960
  716.2 11.0 reduce-scatter.5.cloned.1.call-done
  727.2 6.0 convert_add_fusion
  733.2 137.7 %reduce-scatter.9.cloned.1.call-done = f32[24,3072]{1,0:T(8,128)} async-done(((f32[768,3072]{1,0:T(8,128)}), f32[24,3072]{1,0:T(8,128)}) %reduce-scatter.9.cloned.1.call-update) | async-done | bytes 294928 | tf_op jit(solution)/shard_map/reduce_scatter | solution.py:188
  873.2 138.3 %reduce-scatter.11.cloned.1.call-done = f32[96,768]{1,0:T(8,128)} async-done(((f32[3072,768]{1,0:T(8,128)}), f32[96,768]{1,0:T(8,128)}) %reduce-scatter.11.cloned.1.call-update) | async-done | bytes 294928 | tf_op jit(solution)/shard_map/reduce_scatter | solution.py:189
  1013.9 6.2 copy.158
  1020.1 4.3 all-reduce.2
  1024.4 75.5 %all-reduce.1 = (f32[]{:T(128)}, f32[12,768]{1,0:T(8,128)S(1)}) all-reduce(f32[]{:T(128)} %get-tuple-element.305, f32[12,768]{1,0:T(8,128)} %get-tuple-element.306), channel_id=1, replica_groups=mesh['rows'=16,'heads'=2] {'rows'}, use_global_device_ids=true, to_apply=%region_25.26 | all-reduce | flops 9217 | bytes 73736 | tf_op jit(solution)/shard_map/psum | solution.py:20
  (255 shorter events, 168.0 us)
Async XLA Ops:
  7.2 65.8 %all-gather.5.cloned.1.call-start = ((), (), s32[]{:S(2)}) async-start(), calls=%async_computation.6 | async-start | bytes 1880064 | tf_op jit(solution)/shard_map/all_gather | solution.py:120
  8.9 190.9 %all-gather.7.cloned.1.call-start = ((), (), s32[]{:S(2)}) async-start(), calls=%async_computation.7 | async-start | bytes 1216512 | tf_op jit(solution)/shard_map/all_gather | solution.py:122
  10.4 199.9 %all-gather.9.cloned.1.call-start = ((), (), s32[]{:S(2)}) async-start(), calls=%async_computation.8 | async-start | bytes 4866048 | tf_op jit(solution)/shard_map/all_gather | solution.py:123
  12.2 249.2 %all-gather.11.cloned.1.call-start = ((), (), s32[]{:S(2)}) async-start(), calls=%async_computation.9 | async-start | bytes 4866048 | tf_op jit(solution)/shard_map/all_gather | solution.py:124
  15.6 245.8 %copy-start.29 = (f32[768]{0:T(1024)}, f32[768]{0:T(1024)S(1)}, u32[]{:S(2)}) copy-start(f32[768]{0:T(1024)S(1)} %get-tuple-element.265) | copy-start | bytes 9220
  15.8 4.3 slice-start.4
  117.3 5.8 copy-start.39
  178.8 12.5 %copy-start.3 = (bf16[6,512,6,64]{1,3,2,0:T(8,128)(2,1)}, bf16[6,512,6,64]{1,3,2,0:T(8,128)(2,1)S(1)}, u32[]{:S(2)}) copy-start(bf16[6,512,6,64]{1,3,2,0:T(8,128)(2,1)S(1)} %get-tuple-element.531) | copy-start | bytes 7077892
  194.7 8.2 copy-start.6
  194.7 8.2 all-to-all-start
  199.7 384.1 %reduce-scatter.7.cloned.1.call-start = ((), (), s32[]{:S(2)}) async-start(), calls=%async_computation.11 | async-start | bytes 2433024 | tf_op jit(solution)/shard_map/reduce_scatter | solution.py:187
  207.3 2.2 copy-start.1
  207.9 1.0 copy-start.21
  210.3 51.1 %copy-start.36 = (f32[768]{0:T(1024)S(1)}, f32[768]{0:T(1024)}, u32[]{:S(2)}) copy-start(f32[768]{0:T(1024)} %get-tuple-element.264) | copy-start | bytes 9220
  261.3 13.7 %copy-start.2 = (bf16[1536,768]{0,1:T(8,128)(2,1)S(1)}, bf16[1536,768]{0,1:T(8,128)(2,1)}, u32[]{:S(2)}) copy-start(bf16[1536,768]{0,1:T(8,128)(2,1)} %copy.140) | copy-start | bytes 7077892
  261.3 13.7 %copy-start.27 = (f32[768]{0:T(1024)S(1)}, f32[768]{0:T(1024)}, u32[]{:S(2)}) copy-start(f32[768]{0:T(1024)} %get-tuple-element.263) | copy-start | bytes 9220
  277.1 3.1 copy-start.31
  280.2 32.2 %slice-start = ((s8[4718592]{0:T(1024)(128)(4,1)}), s8[4194304]{0:T(1024)(128)(4,1)S(1)}, s32[]{:S(2)}) async-start(s8[4718592]{0:T(1024)(128)(4,1)} %bitcast.159), calls=%async_computation.15 | async-start | bytes 8388608
  285.6 26.8 %slice-start.1 = ((s8[4718592]{0:T(1024)(128)(4,1)}), s8[524288]{0:T(1024)(128)(4,1)S(1)}, s32[]{:S(2)}) async-start(s8[4718592]{0:T(1024)(128)(4,1)} %bitcast.159), calls=%async_computation.16 | async-start | bytes 1048576
  312.4 14.9 %copy-start.22 = (f32[1536]{0:T(1024)S(1)}, f32[1536]{0:T(1024)}, u32[]{:S(2)}) copy-start(f32[1536]{0:T(1024)} %copy-done.21) | copy-start | bytes 18436
  328.7 2.2 copy-start
  328.7 8.3 copy-start.25
  357.6 3.7 copy-start.40
  357.6 355.5 %all-reduce.5.cloned.1.call-start = ((), (), s32[]{:S(2)}) async-start(), calls=%async_computation.14 | async-start | bytes 9437184
  514.0 2.4 copy-start.4
  514.0 3.1 copy-start.5
  514.0 6.5 slice-start.2
  516.4 4.1 slice-start.3
  517.5 2.9 copy-start.12
  534.5 192.7 %reduce-scatter.5.cloned.1.call-start = ((), (), s32[]{:S(2)}) async-start(), calls=%async_computation.10 | async-start | bytes 7077888 | tf_op jit(solution)/shard_map/reduce_scatter | solution.py:182
  545.0 0.7 copy-start.30
  545.1 325.8 %reduce-scatter.9.cloned.1.call-start = ((), (), s32[]{:S(2)}) async-start(), calls=%async_computation.12 | async-start | bytes 9732096 | tf_op jit(solution)/shard_map/reduce_scatter | solution.py:188
  559.6 451.9 %reduce-scatter.11.cloned.1.call-start = ((), (), s32[]{:S(2)}) async-start(), calls=%async_computation.13 | async-start | bytes 9732096 | tf_op jit(solution)/shard_map/reduce_scatter | solution.py:189
  572.9 0.7 copy-start.41
  572.9 4.5 copy-start.34
  573.0 4.5 copy-start.38
  573.0 4.5 copy-start.37
  573.0 4.5 copy-start.35
  573.0 4.6 copy-start.33
  573.0 4.6 copy-start.32
  573.0 4.6 copy-start.28
  577.6 149.6 %copy-start.26 = (f32[1536]{0:T(1024)S(1)}, f32[1536]{0:T(1024)}, u32[]{:S(2)}) copy-start(f32[1536]{0:T(1024)} %copy-done.25) | copy-start | bytes 18436
  1013.8 89.7 %copy-start.11 = (f32[3,48,384]{2,1,0:T(8,128)S(1)}, f32[3,48,384]{2,1,0:T(8,128)}, u32[]{:S(2)}) copy-start(f32[3,48,384]{2,1,0:T(8,128)} %param.25) | copy-start | bytes 663556
  1013.8 89.6 %copy-start.19 = (f32[3,48,384]{2,1,0:T(8,128)S(1)}, f32[3,48,384]{2,1,0:T(8,128)}, u32[]{:S(2)}) copy-start(f32[3,48,384]{2,1,0:T(8,128)} %param.26) | copy-start | bytes 663556
  1013.8 89.6 %copy-start.20 = (f32[3,48,384]{2,1,0:T(8,128)S(1)}, f32[3,48,384]{2,1,0:T(8,128)}, u32[]{:S(2)}) copy-start(f32[3,48,384]{2,1,0:T(8,128)} %param.27) | copy-start | bytes 663556
  1013.8 90.6 %copy-start.7 = (f32[96,768]{1,0:T(8,128)S(1)}, f32[96,768]{1,0:T(8,128)}, u32[]{:S(2)}) copy-start(f32[96,768]{1,0:T(8,128)} %param.34) | copy-start | bytes 884740
  1013.8 90.6 %copy-start.10 = (f32[96,768]{1,0:T(8,128)S(1)}, f32[96,768]{1,0:T(8,128)}, u32[]{:S(2)}) copy-start(f32[96,768]{1,0:T(8,128)} %reduce-scatter.11.cloned.1.call-done) | copy-start | bytes 884740
  1013.8 90.6 %copy-start.13 = (f32[96,768]{1,0:T(8,128)S(1)}, f32[96,768]{1,0:T(8,128)}, u32[]{:S(2)}) copy-start(f32[96,768]{1,0:T(8,128)} %param.35) | copy-start | bytes 884740
  1013.8 90.6 %copy-start.14 = (f32[96,768]{1,0:T(8,128)S(1)}, f32[96,768]{1,0:T(8,128)}, u32[]{:S(2)}) copy-start(f32[96,768]{1,0:T(8,128)} %param.36) | copy-start | bytes 884740
  1013.8 91.6 %copy-start.8 = (f32[24,3072]{1,0:T(8,128)S(1)}, f32[24,3072]{1,0:T(8,128)}, u32[]{:S(2)}) copy-start(f32[24,3072]{1,0:T(8,128)} %param.31) | copy-start | bytes 884740
  1013.8 91.6 %copy-start.9 = (f32[24,3072]{1,0:T(8,128)S(1)}, f32[24,3072]{1,0:T(8,128)}, u32[]{:S(2)}) copy-start(f32[24,3072]{1,0:T(8,128)} %reduce-scatter.9.cloned.1.call-done) | copy-start | bytes 884740
  1013.9 91.6 %copy-start.15 = (f32[24,3072]{1,0:T(8,128)S(1)}, f32[24,3072]{1,0:T(8,128)}, u32[]{:S(2)}) copy-start(f32[24,3072]{1,0:T(8,128)} %param.32) | copy-start | bytes 884740
  1013.9 91.6 %copy-start.16 = (f32[24,3072]{1,0:T(8,128)S(1)}, f32[24,3072]{1,0:T(8,128)}, u32[]{:S(2)}) copy-start(f32[24,3072]{1,0:T(8,128)} %param.33) | copy-start | bytes 884740
  1020.1 86.4 %copy-start.17 = (f32[24,768]{1,0:T(8,128)S(1)}, f32[24,768]{1,0:T(8,128)}, u32[]{:S(2)}) copy-start(f32[24,768]{1,0:T(8,128)} %param.28) | copy-start | bytes 221188
  1020.1 86.4 %copy-start.18 = (f32[24,768]{1,0:T(8,128)S(1)}, f32[24,768]{1,0:T(8,128)}, u32[]{:S(2)}) copy-start(f32[24,768]{1,0:T(8,128)} %reduce-scatter.7.cloned.1.call-done) | copy-start | bytes 221188
  1101.8 4.7 copy-start.23
  1101.8 4.7 copy-start.24
Sparse Core Ops, SparseCore 0:
  11.3 61.6 all-gather.4
  76.4 52.7 all-gather.6
  132.8 62.5 all-gather.8
  198.7 62.6 all-gather.10
  357.8 97.8 reduce-scatter.6
  534.6 178.5 all-reduce.4
  715.5 11.6 reduce-scatter.4
  734.1 136.7 reduce-scatter.8
  876.8 134.5 reduce-scatter.10
